TPU v7x, 128 devices: a whole 4x4x4 slice. The times are simulated.
128 devices in a mesh: dp: 64 (over y_hi, z, x, core), col: 2 (over y_lo).
Axes of the slice: x: 4, y: 4 (y_hi: 2, y_lo: 2; y = y_hi * 2 + y_lo), z: 4, core: 2. Of those that a mesh axis runs over, the one named last changes fastest.
Arguments:
- tokens: bfloat16 [8192, 2048], P('dp'), may hold values from -6 to 6
- routes: int32 [8192, 8], P('dp'), may hold values from 0 to 127, all different within a row; in each aligned block of 128 rows (0 to 127, 128 to 255, ...) at most 12 rows name the same one
- probs: float32 [8192, 8], P('dp'), may hold values from 0.1 to 1
- w_gate: bfloat16 [128, 2048, 768], P('dp', None, 'col'), may hold values from -0.125 to 0.125
- w_up: bfloat16 [128, 2048, 768], P('dp', None, 'col'), may hold values from -0.125 to 0.125
- w_down: bfloat16 [128, 768, 2048], P('dp', 'col'), may hold values from -0.21875 to 0.21875
- cotangent: bfloat16 [8192, 2048], P('dp', 'col'), may hold values from -6 to 6
Outputs:
- mixed: bfloat16 [8192, 2048], P('dp', 'col')
- grad_tokens: bfloat16 [8192, 2048], P('dp', 'col')
- grad_probs: float32 [8192, 8], P('dp')
- grad_gate: bfloat16 [128, 2048, 768], P('dp', None, 'col')
- grad_up: bfloat16 [128, 2048, 768], P('dp', None, 'col')
- grad_down: bfloat16 [128, 768, 2048], P('dp', 'col')
Inputs may be any that keep to these rules, and one draw needn't show every extreme that they name: `routes`: each token names 8 different experts. Among the 128 tokens of one index of dp, no expert is named by more than 12 of them, a bound that some block reaches.
All inputs are finite; a program needn't handle non-finite values.
Results may differ from a plain program's by a relative error of at most 0.0064.
Values may be sent and summed in bfloat16 or wider, within the bound.
A program may use at most 192 MiB of HBM per device.

v0:
```python
import jax
import jax.numpy as jnp
from jax import lax
from jax.sharding import PartitionSpec as P


def body(tokens, routes, probs, w_gate, w_up, w_down, cotangent):
    tok_count, width = tokens.shape
    top_count = routes.shape[1]
    owners = lax.axis_size("dp")
    cols = lax.axis_size("col")
    local_experts = w_gate.shape[0]
    experts = local_experts * owners
    slot_cap = 3 * tok_count * top_count // (2 * experts)
    half_width = width // cols
    pair_count = tok_count * top_count
    rows_per_owner = local_experts * slot_cap
    slots = experts * slot_cap
    flat_routes = routes.reshape(-1)
    expert_ids = jnp.arange(experts, dtype=jnp.int32)
    onehot = (flat_routes[:, None] == expert_ids[None, :]).astype(jnp.int32)
    before = jnp.cumsum(onehot, axis=0) - onehot
    slot_index = jnp.sum(before * onehot, axis=1)
    flat_index = flat_routes * slot_cap + slot_index
    slot_ids = jnp.arange(slots, dtype=jnp.int32)
    match = flat_index.reshape(tok_count, top_count)[:, :, None] == slot_ids[None, None, :]
    weight = jnp.sum(jnp.where(match, probs[:, :, None], 0.0), axis=1)
    taken = jnp.any(match, axis=1)
    picker = taken.astype(jnp.bfloat16)
    weight_hi = weight.astype(jnp.bfloat16)
    weight_lo = (weight - weight_hi.astype(jnp.float32)).astype(jnp.bfloat16)
    prob_of_slot = jnp.sum(weight, axis=0)
    both = ("dp", "col")
    col_me = lax.axis_index("col")
    tok_half = lax.dynamic_slice_in_dim(tokens, col_me * half_width, half_width, axis=1)
    tok_rows = jnp.einsum("ts,td->sd", picker, tok_half, preferred_element_type=jnp.float32)
    cot_rows = jnp.einsum("ts,td->sd", picker, cotangent, preferred_element_type=jnp.float32)

    def spread(rows_half):
        return jnp.broadcast_to(
            rows_half.reshape(owners, 1, rows_per_owner, half_width),
            (owners, cols, rows_per_owner, half_width),
        ).reshape(owners * cols, rows_per_owner, half_width)

    def dispatch(sent):
        got = lax.all_to_all(sent, both, 0, 0, tiled=True)
        return got.reshape(owners, cols, rows_per_owner, half_width)

    tok_sent, cot_sent = lax.optimization_barrier(
        (
            spread(tok_rows.astype(jnp.bfloat16)),
            spread((prob_of_slot[:, None] * cot_rows).astype(jnp.bfloat16)),
        )
    )
    row_block = dispatch(tok_sent)
    d_out = dispatch(cot_sent)
    w_gate_h = w_gate.reshape(local_experts, cols, half_width, -1)
    w_up_h = w_up.reshape(local_experts, cols, half_width, -1)
    w_down_h = w_down.reshape(local_experts, w_down.shape[1], cols, half_width)
    expert_of_row = jnp.arange(rows_per_owner, dtype=jnp.int32) // slot_cap
    own = (expert_of_row[:, None] == jnp.arange(local_experts, dtype=jnp.int32)[None, :])[
        None, :, :, None
    ]

    def per_half(table):
        return jnp.broadcast_to(
            table.reshape(tok_count, owners, 1, rows_per_owner),
            (tok_count, owners, cols, rows_per_owner),
        )

    def send_back(halves):
        part = jnp.stack([h.astype(jnp.bfloat16) for h in halves], axis=1)
        got = lax.all_to_all(
            part.reshape(owners * cols, rows_per_owner, half_width), both, 0, 0, tiled=True
        )
        return got.reshape(owners, cols, rows_per_owner, half_width)

    def flat(got):
        return got.reshape(owners * cols * rows_per_owner, half_width)

    def combine(table, got):
        lhs = per_half(table).reshape(tok_count, owners * cols * rows_per_owner)
        return jnp.dot(lhs, flat(got), preferred_element_type=jnp.float32)

    def halves_of(ref, axis):
        return [
            lax.slice_in_dim(ref, j * half_width, (j + 1) * half_width, axis=axis)
            for j in range(cols)
        ]

    gate_acts = jnp.einsum(
        "scrd,lcdh->srlh", row_block, w_gate_h, preferred_element_type=jnp.float32
    )
    up_acts = jnp.einsum("scrd,lcdh->srlh", row_block, w_up_h, preferred_element_type=jnp.float32)
    gate_acts = jnp.where(own, gate_acts, 0.0)
    up_acts = jnp.where(own, up_acts, 0.0)
    sigmoid_g = jax.nn.sigmoid(gate_acts)
    silu_g = gate_acts * sigmoid_g
    hidden = (silu_g * up_acts).astype(jnp.bfloat16)
    out_halves = [
        jnp.einsum("srlh,lhd->srd", hidden, w, preferred_element_type=jnp.float32)
        for w in halves_of(w_down, 2)
    ]
    d_out, out_halves = lax.optimization_barrier((d_out, out_halves))
    got_out = send_back(out_halves)
    stacked = jnp.broadcast_to(
        jnp.stack([weight_hi, weight_lo]).reshape(2, tok_count, owners, 1, rows_per_owner),
        (2, tok_count, owners, cols, rows_per_owner),
    )
    both_parts = jnp.dot(
        stacked.reshape(2 * tok_count, owners * cols * rows_per_owner),
        flat(got_out),
        preferred_element_type=jnp.float32,
    )
    mixed = (both_parts[:tok_count] + both_parts[tok_count:]).astype(jnp.bfloat16)
    dots = lax.dot_general(
        cotangent, flat(got_out), (((1,), (1,)), ((), ())), preferred_element_type=jnp.float32
    ).reshape(tok_count, owners, cols, rows_per_owner)
    dots = jnp.sum(dots, axis=2).reshape(tok_count, 1, slots)
    prob_part = jnp.sum(jnp.where(match, dots, 0.0), axis=2)
    grad_down = (
        jnp.einsum("srlh,scrd->lhcd", hidden, d_out, preferred_element_type=jnp.float32)
        .astype(jnp.bfloat16)
        .reshape(w_down.shape)
    )
    d_hidden = jnp.einsum("scrd,lhcd->srlh", d_out, w_down_h, preferred_element_type=jnp.float32)
    d_hidden = jnp.where(own, d_hidden, 0.0)
    d_gate = (d_hidden * up_acts * sigmoid_g * (1.0 + gate_acts * (1.0 - sigmoid_g))).astype(
        jnp.bfloat16
    )
    d_up = (d_hidden * silu_g).astype(jnp.bfloat16)
    grad_gate = (
        jnp.einsum("scrd,srlh->lcdh", row_block, d_gate, preferred_element_type=jnp.float32)
        .astype(jnp.bfloat16)
        .reshape(w_gate.shape)
    )
    grad_up = (
        jnp.einsum("scrd,srlh->lcdh", row_block, d_up, preferred_element_type=jnp.float32)
        .astype(jnp.bfloat16)
        .reshape(w_up.shape)
    )
    got_grad = send_back(
        [
            jnp.einsum("srlh,ldh->srd", d_gate, wg, preferred_element_type=jnp.float32)
            + jnp.einsum("srlh,ldh->srd", d_up, wu, preferred_element_type=jnp.float32)
            for wg, wu in zip(halves_of(w_gate, 1), halves_of(w_up, 1))
        ]
    )
    grad_tokens = combine(picker, got_grad).astype(jnp.bfloat16)
    prob_part, mixed = lax.optimization_barrier((prob_part, mixed))
    grad_probs = lax.psum(prob_part, "col")
    return (mixed, grad_tokens, grad_probs, grad_gate, grad_up, grad_down)


def solution(mesh):
    return jax.shard_map(
        body,
        mesh=mesh,
        in_specs=(
            P("dp", None),
            P("dp", None),
            P("dp", None),
            P("dp", None, "col"),
            P("dp", None, "col"),
            P("dp", "col", None),
            P("dp", "col"),
        ),
        out_specs=(
            P("dp", "col"),
            P("dp", "col"),
            P("dp", None),
            P("dp", None, "col"),
            P("dp", None, "col"),
            P("dp", "col", None),
        ),
        check_vma=False,
    )
```

profile of v0, /device:TPU:82, one launch (start us, length us, event | category | flops | bytes accessed | tf_op | source)
XLA Modules:
  0.0 381.2 jit_solution(2753015450887470145)
XLA Ops:
  3.7 3.1 fusion.11
  6.8 2.5 select_reduce_fusion
  11.4 3.4 broadcast_in_dim.86
  15.8 80.2 %all_to_all.20 = bf16[128,24,1024]{2,1,0:T(8,128)(2,1)} all-to-all(bf16[128,24,1024]{2,1,0:T(8,128)(2,1)S(1)} %bitcast.215), channel_id=1, replica_groups=mesh['dp'=64,'col'=2] {'dp','col'}, dimensions={0} | all-to-all | bytes 12582912 | tf_op jit(solution)/shard_map/all_to_all | solution.py:46
  95.9 11.4 %all-to-all-start = ((bf16[128,24,1024]{2,1,0:T(8,128)(2,1)}), bf16[128,24,1024]{2,1,0:T(8,128)(2,1)}, u32[]{:S(2)}, u32[]{:S(2)}) async-start(bf16[128,24,1024]{2,1,0:T(8,128)(2,1)} %bitcast.212), calls=%async_computation | async-start | bytes 12582912 | tf_op jit(solution)/shard_map/all_to_all | solution.py:46
  110.6 7.7 %fusion.60 = f32[64,24,2,384,1]{3,1,4,2,0:T(8,128)S(1)} fusion(bf16[64,2,24,1024,1]{3,2,1,4,0:T(8,128)(2,1)} %bitcast.221, bf16[2,2,1024,384,1]{3,2,1,0,4:T(8,128)(2,1)S(1)} %bitcast.238), kind=kOutput, calls=%fused_computation.88 | convolution fusion | flops 4831838208 | bytes 14155776 | tf_op jit(solution)/shard_map/scrd,lcdh->srlh/dot_general | solution.py:91
  118.4 7.4 %multiply_convert_fusion.3 = (bf16[64,24,2,384]{3,1,2,0:T(8,128)(2,1)S(1)}, f32[64,24,2,384,1]{3,1,4,2,0:T(8,128)}) fusion(pred[24,2]{0,1:T(4,128)(4,1)S(1)} %iota_compare_fusion.4, f32[64,24,2,384,1]{3,1,4,2,0:T(8,128)S(1)} %fusion.60, bf16[64,2,24,1024,1]{3,2,1,4,0:T(8,128)(2,1)S(1)} %bitcast.225, bf16[2,2,1024,384,1]{3,2,1,0,4:T(8,128)(2,1)S(1)} %bitcast.239), kind=kOutput, calls=%fused_computation.31 | convolution fusion | flops 4841275392 | bytes 21233712 | tf_op jit(solution)/shard_map/scrd,lcdh->srlh/dot_general | solution.py:94
  125.8 4.0 %convolution_bitcast_fusion = bf16[64,24,1024]{2,1,0:T(8,128)(2,1)} fusion(bf16[64,24,2,384]{3,1,2,0:T(8,128)(2,1)S(1)} %get-tuple-element.44, bf16[2,384,2048]{2,1,0:T(8,128)(2,1)S(1)} %copy-done.8), kind=kOutput, calls=%fused_computation.43 | convolution fusion | flops 2415919104 | bytes 7077888 | tf_op jit(solution)/shard_map/srlh,lhd->srd/dot_general | solution.py:101
  129.8 4.0 %convolution_bitcast_fusion.1 = bf16[64,24,1024]{2,1,0:T(8,128)(2,1)} fusion(bf16[64,24,2,384]{3,1,2,0:T(8,128)(2,1)S(1)} %get-tuple-element.44, bf16[2,384,2048]{2,1,0:T(8,128)(2,1)S(1)} %copy-done.8), kind=kOutput, calls=%fused_computation.44 | convolution fusion | flops 2415919104 | bytes 7077888 | tf_op jit(solution)/shard_map/srlh,lhd->srd/dot_general | solution.py:101
  133.8 52.4 %all-to-all-done = bf16[128,24,1024]{2,1,0:T(8,128)(2,1)} async-done(((bf16[128,24,1024]{2,1,0:T(8,128)(2,1)}), bf16[128,24,1024]{2,1,0:T(8,128)(2,1)}, u32[]{:S(2)}, u32[]{:S(2)}) %all-to-all-start) | async-done | bytes 6291488 | tf_op jit(solution)/shard_map/all_to_all | solution.py:46
  186.2 3.4 pad_maximum_fusion
  189.6 3.3 copy.76
  192.9 10.1 %all-to-all-start.2 = ((bf16[128,24,1024]{2,1,0:T(8,128)(2,1)}), bf16[128,24,1024]{2,1,0:T(8,128)(2,1)}, u32[]{:S(2)}, u32[]{:S(2)}) async-start(bf16[128,24,1024]{2,1,0:T(8,128)(2,1)} %bitcast.213), calls=%async_computation.2 | async-start | bytes 12582912 | tf_op jit(solution)/shard_map/all_to_all | solution.py:73
  203.0 9.3 %bitcast_convert_fusion = bf16[2,384,2,1024]{3,1,2,0:T(8,128)(2,1)} fusion(bf16[64,2,24,1024]{3,2,1,0:T(8,128)(2,1)} %bitcast.7, bf16[64,24,2,384]{3,1,2,0:T(8,128)(2,1)S(1)} %get-tuple-element.44), kind=kOutput, calls=%fused_computation.6 | convolution fusion | flops 4833411072 | bytes 11796480 | tf_op jit(solution)/shard_map/srlh,scrd->lhcd/dot_general | solution.py:122
  212.3 4.6 %copy.91 = bf16[2,384,2,1024]{1,3,2,0:T(8,128)(2,1)} copy(bf16[2,384,2,1024]{3,1,2,0:T(8,128)(2,1)} %bitcast_convert_fusion) | data formatting | bytes 6291456 | tf_op jit(solution)/shard_map/convert_element_type | solution.py:123
  216.9 4.8 %copy.93 = bf16[2,384,2048]{2,1,0:T(8,128)(2,1)} copy(bf16[2,384,2048]{1,2,0:T(8,128)(2,1)} %bitcast.217) | data formatting | bytes 6291456
  221.7 14.8 %multiply_convert_fusion.1 = (bf16[64,24,2,384]{3,1,2,0:T(8,128)(2,1)}, bf16[64,24,2,384]{3,1,2,0:T(8,128)(2,1)S(1)}) fusion(pred[24,2]{0,1:T(4,128)(4,1)S(1)} %iota_compare_fusion.4, f32[64,24,2,384,1]{3,1,4,2,0:T(8,128)} %copy-done.17, f32[64,24,2,384,1]{3,1,4,2,0:T(8,128)} %get-tuple-element.45, bf16[2,48,2,8,1024]{4,3,2,1,0:T(8,128)(2,1)} %bitcast.237, ...), kind=kOutput, calls=%fused_computation.29 | convolution fusion | flops 4850712576 | bytes 23593008 | tf_op jit(solution)/shard_map/scrd,lhcd->srlh/dot_general | solution.py:126
  237.9 6.5 %fusion.17 = bf16[2,2,1024,384]{2,3,1,0:T(8,128)(2,1)} fusion(bf16[64,2,24,1024]{3,2,1,0:T(8,128)(2,1)S(1)} %bitcast.228, bf16[64,24,2,384]{3,1,2,0:T(8,128)(2,1)S(1)} %get-tuple-element.43), kind=kOutput, calls=%fused_computation.37 | convolution fusion | flops 4833411072 | bytes 11796480 | tf_op jit(solution)/shard_map/scrd,srlh->lcdh/dot_general | solution.py:133
  244.4 5.2 %copy.85 = bf16[2,2,1024,384]{3,2,1,0:T(8,128)(2,1)} copy(bf16[2,2,1024,384]{2,3,1,0:T(8,128)(2,1)} %fusion.17) | data formatting | bytes 6291456 | tf_op jit(solution)/shard_map/convert_element_type | solution.py:134
  249.6 4.3 %fusion.39 = f32[64,24,1024,1]{2,1,3,0:T(8,128)S(1)} fusion(bf16[64,24,2,384]{3,1,2,0:T(8,128)(2,1)S(1)} %copy-done.15, bf16[2,2048,384]{2,1,0:T(8,128)(2,1)} %param.10), kind=kOutput, calls=%fused_computation.52 | convolution fusion | flops 2415919104 | bytes 10223616 | tf_op jit(solution)/shard_map/srlh,ldh->srd/dot_general | solution.py:144
  253.9 2.7 fusion.42
  256.6 3.1 fusion.16
  259.8 3.1 fusion.15
  263.5 3.3 copy.82
  266.8 14.9 %all-to-all-done.2 = bf16[128,24,1024]{2,1,0:T(8,128)(2,1)} async-done(((bf16[128,24,1024]{2,1,0:T(8,128)(2,1)}), bf16[128,24,1024]{2,1,0:T(8,128)(2,1)}, u32[]{:S(2)}, u32[]{:S(2)}) %all-to-all-start.2) | async-done | bytes 6291488 | tf_op jit(solution)/shard_map/all_to_all | solution.py:73
  281.7 10.0 %all-to-all-start.3 = ((bf16[128,24,1024]{2,1,0:T(8,128)(2,1)}), bf16[128,24,1024]{2,1,0:T(8,128)(2,1)}, u32[]{:S(2)}, u32[]{:S(2)}) async-start(bf16[128,24,1024]{2,1,0:T(8,128)(2,1)} %bitcast.214), calls=%async_computation.3 | async-start | bytes 12582912 | tf_op jit(solution)/shard_map/all_to_all | solution.py:73
  291.8 9.3 %fusion.18 = bf16[2,2,1024,384]{2,3,1,0:T(8,128)(2,1)} fusion(bf16[64,2,24,1024]{3,2,1,0:T(8,128)(2,1)} %bitcast.222, bf16[64,24,2,384]{3,1,2,0:T(8,128)(2,1)S(1)} %copy-done.13), kind=kOutput, calls=%fused_computation.38 | convolution fusion | flops 4833411072 | bytes 11796480 | tf_op jit(solution)/shard_map/scrd,srlh->lcdh/dot_general | solution.py:138
  301.1 4.7 %copy.88 = bf16[2,2,1024,384]{3,2,1,0:T(8,128)(2,1)} copy(bf16[2,2,1024,384]{2,3,1,0:T(8,128)(2,1)} %fusion.18) | data formatting | bytes 6291456 | tf_op jit(solution)/shard_map/convert_element_type | solution.py:139
  305.7 4.6 %fusion.61 = f32[3072,128]{1,0:T(8,128)S(1)} fusion(bf16[3072,1024]{1,0:T(8,128)(2,1)} %bitcast.30, bf16[128,1024]{1,0:T(8,128)(2,1)S(1)} %copy-done.6), kind=kOutput, calls=%fused_computation.89 | convolution fusion | flops 805306368 | bytes 8126464 | tf_op jit(solution)/shard_map/dot_general | solution.py:116
  312.7 4.7 %fusion.35 = f32[256,1024]{1,0:T(8,128)S(1)} fusion(bf16[3072,1024]{1,0:T(8,128)(2,1)} %bitcast.30, bf16[384,8,2,128]{3,2,1,0:T(2,128)(2,1)S(1)} %bitcast.216), kind=kOutput, calls=%fused_computation.48 | convolution fusion | flops 1610612736 | bytes 8912896 | tf_op jit(solution)/shard_map/dot_general | solution.py:110
  319.1 56.5 %psum.7 = f32[128,8]{1,0:T(8,128)S(1)} all-reduce(f32[128,8]{1,0:T(8,128)S(1)} %select_reduce_fusion.2), channel_id=1, replica_groups=mesh['dp'=64,'col'=2] {'col'}, use_global_device_ids=true, to_apply=%region_8.9 | all-reduce | flops 1024 | bytes 8192 | tf_op jit(solution)/shard_map/psum | solution.py:151
  376.4 4.6 %convolution_convert_fusion.1 = bf16[128,1024]{1,0:T(8,128)(2,1)} fusion(bf16[128,3072]{0,1:T(8,128)(2,1)S(1)} %bitcast.230, bf16[3072,1024]{1,0:T(8,128)(2,1)} %bitcast.58), kind=kOutput, calls=%fused_computation.65 | convolution fusion | flops 805437440 | bytes 7340032 | tf_op jit(solution)/shard_map/dot_general | solution.py:83
  (82 shorter events, 16.0 us)
Async XLA Ops:
  0.6 8.6 %copy-start = (bf16[128,2048]{1,0:T(8,128)(2,1)S(1)}, bf16[128,2048]{1,0:T(8,128)(2,1)}, u32[]{:S(2)}) copy-start(bf16[128,2048]{1,0:T(8,128)(2,1)} %param.7) | copy-start | bytes 1572868
  0.6 2.9 copy-start.7
  2.9 7.4 %copy-start.5 = (bf16[128,1024]{1,0:T(8,128)(2,1)S(1)}, bf16[128,1024]{1,0:T(8,128)(2,1)}, u32[]{:S(2)}) copy-start(bf16[128,1024]{1,0:T(8,128)(2,1)} %param.13) | copy-start | bytes 786436
  3.6 7.7 %copy-start.3 = (s32[128,8]{1,0:T(8,128)}, s32[128,8]{1,0:T(8,128)S(1)}, u32[]{:S(2)}) copy-start(s32[128,8]{1,0:T(8,128)S(1)} %copy.74) | copy-start | bytes 12292
  95.9 90.2 %all-to-all-start = ((bf16[128,24,1024]{2,1,0:T(8,128)(2,1)}), bf16[128,24,1024]{2,1,0:T(8,128)(2,1)}, u32[]{:S(2)}, u32[]{:S(2)}) async-start(bf16[128,24,1024]{2,1,0:T(8,128)(2,1)} %bitcast.212), calls=%async_computation | async-start | bytes 12582912 | tf_op jit(solution)/shard_map/all_to_all | solution.py:46
  108.6 2.0 copy-start.9
  108.8 9.5 %slice-start = ((s8[6291456]{0:T(1024)(128)(4,1)}), s8[4194304]{0:T(1024)(128)(4,1)S(1)}, s32[]{:S(2)}) async-start(s8[6291456]{0:T(1024)(128)(4,1)} %bitcast.223), calls=%async_computation.4 | async-start | bytes 8388608
  110.6 7.7 %slice-start.1 = ((s8[6291456]{0:T(1024)(128)(4,1)}), s8[2097152]{0:T(1024)(128)(4,1)S(1)}, s32[]{:S(2)}) async-start(s8[6291456]{0:T(1024)(128)(4,1)} %bitcast.223), calls=%async_computation.5 | async-start | bytes 4194304
  110.6 7.7 %copy-start.11 = (bf16[2,2048,384]{2,1,0:T(8,128)(2,1)S(1)}, bf16[2,2048,384]{2,1,0:T(8,128)(2,1)}, u32[]{:S(2)}) copy-start(bf16[2,2048,384]{2,1,0:T(8,128)(2,1)} %param.11) | copy-start | bytes 9437188
  118.3 7.5 %copy-start.17 = (f32[64,24,2,384,1]{3,1,4,2,0:T(8,128)}, f32[64,24,2,384,1]{3,1,4,2,0:T(8,128)S(1)}, u32[]{:S(2)}) copy-start(f32[64,24,2,384,1]{3,1,4,2,0:T(8,128)S(1)} %fusion.60) | copy-start | bytes 14155780
  118.4 7.4 %copy-start.8 = (bf16[2,384,2048]{2,1,0:T(8,128)(2,1)S(1)}, bf16[2,384,2048]{2,1,0:T(8,128)(2,1)}, u32[]{:S(2)}) copy-start(bf16[2,384,2048]{2,1,0:T(8,128)(2,1)} %param.12) | copy-start | bytes 9437188
  192.9 88.8 %all-to-all-start.2 = ((bf16[128,24,1024]{2,1,0:T(8,128)(2,1)}), bf16[128,24,1024]{2,1,0:T(8,128)(2,1)}, u32[]{:S(2)}, u32[]{:S(2)}) async-start(bf16[128,24,1024]{2,1,0:T(8,128)(2,1)} %bitcast.213), calls=%async_computation.2 | async-start | bytes 12582912 | tf_op jit(solution)/shard_map/all_to_all | solution.py:73
  216.9 21.0 %slice-start.2 = ((s8[6291456]{0:T(1024)(128)(4,1)}), s8[2097152]{0:T(1024)(128)(4,1)S(1)}, s32[]{:S(2)}) async-start(s8[6291456]{0:T(1024)(128)(4,1)} %bitcast.226), calls=%async_computation.6 | async-start | bytes 4194304
  221.7 16.2 %slice-start.3 = ((s8[6291456]{0:T(1024)(128)(4,1)}), s8[4194304]{0:T(1024)(128)(4,1)S(1)}, s32[]{:S(2)}) async-start(s8[6291456]{0:T(1024)(128)(4,1)} %bitcast.226), calls=%async_computation.7 | async-start | bytes 8388608
  236.5 1.4 copy-start.14
  244.4 5.2 %copy-start.15 = (bf16[64,24,2,384]{3,1,2,0:T(8,128)(2,1)S(1)}, bf16[64,24,2,384]{3,1,2,0:T(8,128)(2,1)}, u32[]{:S(2)}) copy-start(bf16[64,24,2,384]{3,1,2,0:T(8,128)(2,1)} %copy-done.14) | copy-start | bytes 7077892
  249.6 4.3 %copy-start.10 = (bf16[2,2048,384]{2,1,0:T(8,128)(2,1)S(1)}, bf16[2,2048,384]{2,1,0:T(8,128)(2,1)}, u32[]{:S(2)}) copy-start(bf16[2,2048,384]{2,1,0:T(8,128)(2,1)} %param.10) | copy-start | bytes 9437188
  249.6 4.3 %copy-start.16 = (bf16[64,24,2,384]{3,1,2,0:T(8,128)(2,1)S(1)}, bf16[64,24,2,384]{3,1,2,0:T(8,128)(2,1)}, u32[]{:S(2)}) copy-start(bf16[64,24,2,384]{3,1,2,0:T(8,128)(2,1)} %copy-done.14) | copy-start | bytes 7077892
  253.9 2.8 copy-start.12
  253.9 2.7 copy-start.13
  281.7 94.5 %all-to-all-start.3 = ((bf16[128,24,1024]{2,1,0:T(8,128)(2,1)}), bf16[128,24,1024]{2,1,0:T(8,128)(2,1)}, u32[]{:S(2)}, u32[]{:S(2)}) async-start(bf16[128,24,1024]{2,1,0:T(8,128)(2,1)} %bitcast.214), calls=%async_computation.3 | async-start | bytes 12582912 | tf_op jit(solution)/shard_map/all_to_all | solution.py:73
  301.1 4.7 %copy-start.6 = (bf16[128,1024]{1,0:T(8,128)(2,1)S(1)}, bf16[128,1024]{1,0:T(8,128)(2,1)}, u32[]{:S(2)}) copy-start(bf16[128,1024]{1,0:T(8,128)(2,1)} %param.13) | copy-start | bytes 786436
  312.7 5.5 %copy-start.4 = (s32[128,8]{1,0:T(8,128)S(1)}, s32[128,8]{1,0:T(8,128)}, u32[]{:S(2)}) copy-start(s32[128,8]{1,0:T(8,128)} %copy-done.3) | copy-start | bytes 12292
  312.7 63.5 %copy-start.2 = (bf16[128,1536]{0,1:T(8,128)(2,1)S(1)}, bf16[128,1536]{0,1:T(8,128)(2,1)}, u32[]{:S(2)}) copy-start(bf16[128,1536]{0,1:T(8,128)(2,1)} %copy.80) | copy-start | bytes 1179652
  376.4 4.6 %copy-start.1 = (bf16[128,2048]{1,0:T(8,128)(2,1)S(1)}, bf16[128,2048]{1,0:T(8,128)(2,1)}, u32[]{:S(2)}) copy-start(bf16[128,2048]{1,0:T(8,128)(2,1)} %param.7) | copy-start | bytes 1572868
where the time goes:
time: 389 us; the launch traced here: 381 us
  blocking collectives  137 us (35%)
  matrix products  92.1 us (24%)
  waiting for transfers between devices  67.3 us (17%)
  local copies, waits for them, and re-layouts  39.9 us (10%)
  starting transfers between devices  31.5 us (8%)
  other arithmetic  12.3 us (3%)
    all_to_all x1, blocking collectives, dispatch(): got = lax.all_to_all(sent, both, 0, 0, tiled=True)  80.2 us
    psum x1, blocking collectives, body(): grad_probs = lax.psum(prob_part, 'col')  56.5 us
    all_to_all x1, waiting for transfers between devices, dispatch(): got = lax.all_to_all(sent, both, 0, 0, tiled=True)  52.4 us
    all_to_all x2, starting transfers between devices, send_back(): lax.all_to_all(part.reshape(owners * cols, rows_per_owner, half_width), b...  20.1 us
    all_to_all x2, waiting for transfers between devices, send_back(): lax.all_to_all(part.reshape(owners * cols, rows_per_owner, half_width), b...  14.9 us
    dot_general x1, matrix products, body(): jnp.einsum('scrd,lhcd->srlh', d_out, w_down_h, preferred_element_type=jnp...  14.8 us
    all_to_all x1, starting transfers between devices, dispatch(): got = lax.all_to_all(sent, both, 0, 0, tiled=True)  11.4 us
    dot_general x1, matrix products, body(): jnp.einsum('srlh,scrd->lhcd', hidden, d_out, preferred_element_type=jnp.f...  9.29 us
  transfers between devices with their start and end apart: 3, of which 2 were waited for; matrix products, arithmetic and copies ran while one was open for 31% of the time, Pallas kernels for 0%

commit v1 on v0

--- a/solution.py
+++ b/solution.py
@@ -1,7 +1,16 @@
+import functools
 import jax
 import jax.numpy as jnp
 from jax import lax
 from jax.sharding import PartitionSpec as P
+
+
+def _follow_copies(mine_x, link_axis):
+    prior = lax.all_gather(mine_x, link_axis).sum(axis=0)
+    return prior
+
+
+move_chunk_up = functools.partial(_follow_copies, link_axis="col")
 
 
 def body(tokens, routes, probs, w_gate, w_up, w_down, cotangent):
@@ -148,7 +157,7 @@
     )
     grad_tokens = combine(picker, got_grad).astype(jnp.bfloat16)
     prob_part, mixed = lax.optimization_barrier((prob_part, mixed))
-    grad_probs = lax.psum(prob_part, "col")
+    grad_probs = move_chunk_up(prob_part)
     return (mixed, grad_tokens, grad_probs, grad_gate, grad_up, grad_down)
 
 

time: 389 us -> 387 us (level)
  the two profiles are of different devices: /device:TPU:82 before, /device:TPU:98 now
where the time goes in v1:
time: 387 us; the launch traced here: 379 us
  blocking collectives  129 us (33%)
  matrix products  92.1 us (24%)
  waiting for transfers between devices  83.4 us (22%)
  local copies, waits for them, and re-layouts  39.9 us (10%)
  starting transfers between devices  21.5 us (6%)
  other arithmetic  12.3 us (3%)
    all_to_all x1, blocking collectives, dispatch(): got = lax.all_to_all(sent, both, 0, 0, tiled=True)  82.9 us
    all_to_all x1, waiting for transfers between devices, dispatch(): got = lax.all_to_all(sent, both, 0, 0, tiled=True)  56 us
    all_gather x1, blocking collectives, _follow_copies(): prior = lax.all_gather(mine_x, link_axis).sum(axis=0)  45.9 us
    all_to_all x2, waiting for transfers between devices, send_back(): lax.all_to_all(part.reshape(owners * cols, rows_per_owner, half_width), b...  27.4 us
    dot_general x1, matrix products, body(): jnp.einsum('scrd,lhcd->srlh', d_out, w_down_h, preferred_element_type=jnp...  14.8 us
    all_to_all x2, starting transfers between devices, send_back(): lax.all_to_all(part.reshape(owners * cols, rows_per_owner, half_width), b...  12.9 us
    dot_general x1, matrix products, body(): jnp.einsum('srlh,scrd->lhcd', hidden, d_out, preferred_element_type=jnp.f...  9.3 us
    dot_general x1, matrix products, body(): jnp.einsum('scrd,srlh->lcdh', row_block, d_up, preferred_element_type=jnp...  9.29 us
  transfers between devices with their start and end apart: 3, of which 3 were waited for; matrix products, arithmetic and copies ran while one was open for 31% of the time, Pallas kernels for 0%

profile of v1, /device:TPU:98, one launch (start us, length us, event | category | flops | bytes accessed | tf_op | source)
XLA Modules:
  0.0 379.4 jit_solution(10619890321689972493)
XLA Ops:
  3.7 3.1 fusion.11
  11.4 3.4 broadcast_in_dim.86
  15.8 82.9 %all_to_all.20 = bf16[128,24,1024]{2,1,0:T(8,128)(2,1)} all-to-all(bf16[128,24,1024]{2,1,0:T(8,128)(2,1)S(1)} %bitcast.216), channel_id=1, replica_groups=mesh['dp'=64,'col'=2] {'dp','col'}, dimensions={0} | all-to-all | bytes 12582912 | tf_op jit(solution)/shard_map/all_to_all | solution.py:55
  98.7 8.6 %all-to-all-start = ((bf16[128,24,1024]{2,1,0:T(8,128)(2,1)}), bf16[128,24,1024]{2,1,0:T(8,128)(2,1)}, u32[]{:S(2)}, u32[]{:S(2)}) async-start(bf16[128,24,1024]{2,1,0:T(8,128)(2,1)} %bitcast.214), calls=%async_computation | async-start | bytes 12582912 | tf_op jit(solution)/shard_map/all_to_all | solution.py:55
  110.5 7.7 %fusion.60 = f32[64,24,2,384,1]{3,1,4,2,0:T(8,128)S(1)} fusion(bf16[64,2,24,1024,1]{3,2,1,4,0:T(8,128)(2,1)} %bitcast.222, bf16[2,2,1024,384,1]{3,2,1,0,4:T(8,128)(2,1)S(1)} %bitcast.240), kind=kOutput, calls=%fused_computation.88 | convolution fusion | flops 4831838208 | bytes 14155776 | tf_op jit(solution)/shard_map/scrd,lcdh->srlh/dot_general | solution.py:100
  118.3 7.4 %multiply_convert_fusion.3 = (bf16[64,24,2,384]{3,1,2,0:T(8,128)(2,1)S(1)}, f32[64,24,2,384,1]{3,1,4,2,0:T(8,128)}) fusion(pred[24,2]{0,1:T(4,128)(4,1)S(1)} %iota_compare_fusion.4, f32[64,24,2,384,1]{3,1,4,2,0:T(8,128)S(1)} %fusion.60, bf16[64,2,24,1024,1]{3,2,1,4,0:T(8,128)(2,1)S(1)} %bitcast.226, bf16[2,2,1024,384,1]{3,2,1,0,4:T(8,128)(2,1)S(1)} %bitcast.241), kind=kOutput, calls=%fused_computation.31 | convolution fusion | flops 4841275392 | bytes 21233712 | tf_op jit(solution)/shard_map/scrd,lcdh->srlh/dot_general | solution.py:103
  125.7 4.0 %convolution_bitcast_fusion = bf16[64,24,1024]{2,1,0:T(8,128)(2,1)} fusion(bf16[64,24,2,384]{3,1,2,0:T(8,128)(2,1)S(1)} %get-tuple-element.44, bf16[2,384,2048]{2,1,0:T(8,128)(2,1)S(1)} %copy-done.8), kind=kOutput, calls=%fused_computation.43 | convolution fusion | flops 2415919104 | bytes 7077888 | tf_op jit(solution)/shard_map/srlh,lhd->srd/dot_general | solution.py:110
  129.7 4.0 %convolution_bitcast_fusion.1 = bf16[64,24,1024]{2,1,0:T(8,128)(2,1)} fusion(bf16[64,24,2,384]{3,1,2,0:T(8,128)(2,1)S(1)} %get-tuple-element.44, bf16[2,384,2048]{2,1,0:T(8,128)(2,1)S(1)} %copy-done.8), kind=kOutput, calls=%fused_computation.44 | convolution fusion | flops 2415919104 | bytes 7077888 | tf_op jit(solution)/shard_map/srlh,lhd->srd/dot_general | solution.py:110
  133.7 56.0 %all-to-all-done = bf16[128,24,1024]{2,1,0:T(8,128)(2,1)} async-done(((bf16[128,24,1024]{2,1,0:T(8,128)(2,1)}), bf16[128,24,1024]{2,1,0:T(8,128)(2,1)}, u32[]{:S(2)}, u32[]{:S(2)}) %all-to-all-start) | async-done | bytes 6291488 | tf_op jit(solution)/shard_map/all_to_all | solution.py:55
  189.7 3.4 pad_maximum_fusion
  193.1 3.3 copy.76
  196.4 6.5 %all-to-all-start.2 = ((bf16[128,24,1024]{2,1,0:T(8,128)(2,1)}), bf16[128,24,1024]{2,1,0:T(8,128)(2,1)}, u32[]{:S(2)}, u32[]{:S(2)}) async-start(bf16[128,24,1024]{2,1,0:T(8,128)(2,1)} %bitcast.215), calls=%async_computation.2 | async-start | bytes 12582912 | tf_op jit(solution)/shard_map/all_to_all | solution.py:82
  202.9 9.3 %bitcast_convert_fusion = bf16[2,384,2,1024]{3,1,2,0:T(8,128)(2,1)} fusion(bf16[64,2,24,1024]{3,2,1,0:T(8,128)(2,1)} %bitcast.7, bf16[64,24,2,384]{3,1,2,0:T(8,128)(2,1)S(1)} %get-tuple-element.44), kind=kOutput, calls=%fused_computation.6 | convolution fusion | flops 4833411072 | bytes 11796480 | tf_op jit(solution)/shard_map/srlh,scrd->lhcd/dot_general | solution.py:131
  212.2 4.6 %copy.92 = bf16[2,384,2,1024]{1,3,2,0:T(8,128)(2,1)} copy(bf16[2,384,2,1024]{3,1,2,0:T(8,128)(2,1)} %bitcast_convert_fusion) | data formatting | bytes 6291456 | tf_op jit(solution)/shard_map/convert_element_type | solution.py:132
  216.8 4.8 %copy.93 = bf16[2,384,2048]{2,1,0:T(8,128)(2,1)} copy(bf16[2,384,2048]{1,2,0:T(8,128)(2,1)} %bitcast.218) | data formatting | bytes 6291456
  221.6 14.8 %multiply_convert_fusion.1 = (bf16[64,24,2,384]{3,1,2,0:T(8,128)(2,1)}, bf16[64,24,2,384]{3,1,2,0:T(8,128)(2,1)S(1)}) fusion(pred[24,2]{0,1:T(4,128)(4,1)S(1)} %iota_compare_fusion.4, f32[64,24,2,384,1]{3,1,4,2,0:T(8,128)} %copy-done.17, f32[64,24,2,384,1]{3,1,4,2,0:T(8,128)} %get-tuple-element.45, bf16[2,48,2,8,1024]{4,3,2,1,0:T(8,128)(2,1)} %bitcast.239, ...), kind=kOutput, calls=%fused_computation.29 | convolution fusion | flops 4850712576 | bytes 23593008 | tf_op jit(solution)/shard_map/scrd,lhcd->srlh/dot_general | solution.py:135
  237.8 6.5 %fusion.17 = bf16[2,2,1024,384]{2,3,1,0:T(8,128)(2,1)} fusion(bf16[64,2,24,1024]{3,2,1,0:T(8,128)(2,1)S(1)} %bitcast.229, bf16[64,24,2,384]{3,1,2,0:T(8,128)(2,1)S(1)} %get-tuple-element.43), kind=kOutput, calls=%fused_computation.37 | convolution fusion | flops 4833411072 | bytes 11796480 | tf_op jit(solution)/shard_map/scrd,srlh->lcdh/dot_general | solution.py:142
  244.3 5.2 %copy.86 = bf16[2,2,1024,384]{3,2,1,0:T(8,128)(2,1)} copy(bf16[2,2,1024,384]{2,3,1,0:T(8,128)(2,1)} %fusion.17) | data formatting | bytes 6291456 | tf_op jit(solution)/shard_map/convert_element_type | solution.py:143
  249.5 4.3 %fusion.39 = f32[64,24,1024,1]{2,1,3,0:T(8,128)S(1)} fusion(bf16[64,24,2,384]{3,1,2,0:T(8,128)(2,1)S(1)} %copy-done.15, bf16[2,2048,384]{2,1,0:T(8,128)(2,1)} %param.10), kind=kOutput, calls=%fused_computation.52 | convolution fusion | flops 2415919104 | bytes 10223616 | tf_op jit(solution)/shard_map/srlh,ldh->srd/dot_general | solution.py:153
  253.8 2.7 fusion.42
  256.6 3.1 fusion.16
  259.7 3.1 fusion.15
  263.4 3.3 copy.82
  266.8 18.5 %all-to-all-done.2 = bf16[128,24,1024]{2,1,0:T(8,128)(2,1)} async-done(((bf16[128,24,1024]{2,1,0:T(8,128)(2,1)}), bf16[128,24,1024]{2,1,0:T(8,128)(2,1)}, u32[]{:S(2)}, u32[]{:S(2)}) %all-to-all-start.2) | async-done | bytes 6291488 | tf_op jit(solution)/shard_map/all_to_all | solution.py:82
  285.2 6.4 %all-to-all-start.3 = ((bf16[128,24,1024]{2,1,0:T(8,128)(2,1)}), bf16[128,24,1024]{2,1,0:T(8,128)(2,1)}, u32[]{:S(2)}, u32[]{:S(2)}) async-start(bf16[128,24,1024]{2,1,0:T(8,128)(2,1)} %bitcast.213), calls=%async_computation.3 | async-start | bytes 12582912 | tf_op jit(solution)/shard_map/all_to_all | solution.py:82
  291.7 9.3 %fusion.18 = bf16[2,2,1024,384]{2,3,1,0:T(8,128)(2,1)} fusion(bf16[64,2,24,1024]{3,2,1,0:T(8,128)(2,1)} %bitcast.223, bf16[64,24,2,384]{3,1,2,0:T(8,128)(2,1)S(1)} %copy-done.13), kind=kOutput, calls=%fused_computation.38 | convolution fusion | flops 4833411072 | bytes 11796480 | tf_op jit(solution)/shard_map/scrd,srlh->lcdh/dot_general | solution.py:147
  301.0 4.7 %copy.89 = bf16[2,2,1024,384]{3,2,1,0:T(8,128)(2,1)} copy(bf16[2,2,1024,384]{2,3,1,0:T(8,128)(2,1)} %fusion.18) | data formatting | bytes 6291456 | tf_op jit(solution)/shard_map/convert_element_type | solution.py:148
  305.6 4.6 %fusion.61 = f32[3072,128]{1,0:T(8,128)S(1)} fusion(bf16[3072,1024]{1,0:T(8,128)(2,1)} %bitcast.30, bf16[128,1024]{1,0:T(8,128)(2,1)S(1)} %copy-done.6), kind=kOutput, calls=%fused_computation.89 | convolution fusion | flops 805306368 | bytes 8126464 | tf_op jit(solution)/shard_map/dot_general | solution.py:125
  312.6 4.7 %fusion.35 = f32[256,1024]{1,0:T(8,128)S(1)} fusion(bf16[3072,1024]{1,0:T(8,128)(2,1)} %bitcast.30, bf16[384,8,2,128]{3,2,1,0:T(2,128)(2,1)S(1)} %bitcast.217), kind=kOutput, calls=%fused_computation.48 | convolution fusion | flops 1610612736 | bytes 8912896 | tf_op jit(solution)/shard_map/dot_general | solution.py:119
  319.0 45.9 %all-gather = f32[256,8]{1,0:T(8,128)S(1)} all-gather(f32[128,8]{1,0:T(8,128)S(1)} %select_reduce_fusion.2), channel_id=2, replica_groups=mesh['dp'=64,'col'=2] {'col'}, dimensions={0}, use_global_device_ids=true | all-gather | bytes 12288 | tf_op jit(solution)/shard_map/all_gather | solution.py:9
  365.6 8.9 %all-to-all-done.3 = bf16[128,24,1024]{2,1,0:T(8,128)(2,1)} async-done(((bf16[128,24,1024]{2,1,0:T(8,128)(2,1)}), bf16[128,24,1024]{2,1,0:T(8,128)(2,1)}, u32[]{:S(2)}, u32[]{:S(2)}) %all-to-all-start.3) | async-done | bytes 6291488 | tf_op jit(solution)/shard_map/all_to_all | solution.py:82
  374.6 4.6 %convolution_convert_fusion.1 = bf16[128,1024]{1,0:T(8,128)(2,1)} fusion(bf16[128,3072]{0,1:T(8,128)(2,1)S(1)} %bitcast.230, bf16[3072,1024]{1,0:T(8,128)(2,1)} %bitcast.58), kind=kOutput, calls=%fused_computation.65 | convolution fusion | flops 805437440 | bytes 7340032 | tf_op jit(solution)/shard_map/dot_general | solution.py:92
  (83 shorter events, 18.4 us)
Async XLA Ops:
  0.6 8.6 %copy-start = (bf16[128,2048]{1,0:T(8,128)(2,1)S(1)}, bf16[128,2048]{1,0:T(8,128)(2,1)}, u32[]{:S(2)}) copy-start(bf16[128,2048]{1,0:T(8,128)(2,1)} %param.7) | copy-start | bytes 1572868
  0.6 2.9 copy-start.7
  2.9 7.4 %copy-start.5 = (bf16[128,1024]{1,0:T(8,128)(2,1)S(1)}, bf16[128,1024]{1,0:T(8,128)(2,1)}, u32[]{:S(2)}) copy-start(bf16[128,1024]{1,0:T(8,128)(2,1)} %param.13) | copy-start | bytes 786436
  3.6 7.7 %copy-start.3 = (s32[128,8]{1,0:T(8,128)}, s32[128,8]{1,0:T(8,128)S(1)}, u32[]{:S(2)}) copy-start(s32[128,8]{1,0:T(8,128)S(1)} %copy.74) | copy-start | bytes 12292
  98.7 91.0 %all-to-all-start = ((bf16[128,24,1024]{2,1,0:T(8,128)(2,1)}), bf16[128,24,1024]{2,1,0:T(8,128)(2,1)}, u32[]{:S(2)}, u32[]{:S(2)}) async-start(bf16[128,24,1024]{2,1,0:T(8,128)(2,1)} %bitcast.214), calls=%async_computation | async-start | bytes 12582912 | tf_op jit(solution)/shard_map/all_to_all | solution.py:55
  108.5 2.0 copy-start.9
  108.7 9.5 %slice-start = ((s8[6291456]{0:T(1024)(128)(4,1)}), s8[4194304]{0:T(1024)(128)(4,1)S(1)}, s32[]{:S(2)}) async-start(s8[6291456]{0:T(1024)(128)(4,1)} %bitcast.224), calls=%async_computation.4 | async-start | bytes 8388608
  110.5 7.7 %slice-start.1 = ((s8[6291456]{0:T(1024)(128)(4,1)}), s8[2097152]{0:T(1024)(128)(4,1)S(1)}, s32[]{:S(2)}) async-start(s8[6291456]{0:T(1024)(128)(4,1)} %bitcast.224), calls=%async_computation.5 | async-start | bytes 4194304
  110.5 7.7 %copy-start.11 = (bf16[2,2048,384]{2,1,0:T(8,128)(2,1)S(1)}, bf16[2,2048,384]{2,1,0:T(8,128)(2,1)}, u32[]{:S(2)}) copy-start(bf16[2,2048,384]{2,1,0:T(8,128)(2,1)} %param.11) | copy-start | bytes 9437188
  118.2 7.5 %copy-start.17 = (f32[64,24,2,384,1]{3,1,4,2,0:T(8,128)}, f32[64,24,2,384,1]{3,1,4,2,0:T(8,128)S(1)}, u32[]{:S(2)}) copy-start(f32[64,24,2,384,1]{3,1,4,2,0:T(8,128)S(1)} %fusion.60) | copy-start | bytes 14155780
  118.3 7.4 %copy-start.8 = (bf16[2,384,2048]{2,1,0:T(8,128)(2,1)S(1)}, bf16[2,384,2048]{2,1,0:T(8,128)(2,1)}, u32[]{:S(2)}) copy-start(bf16[2,384,2048]{2,1,0:T(8,128)(2,1)} %param.12) | copy-start | bytes 9437188
  196.4 88.8 %all-to-all-start.2 = ((bf16[128,24,1024]{2,1,0:T(8,128)(2,1)}), bf16[128,24,1024]{2,1,0:T(8,128)(2,1)}, u32[]{:S(2)}, u32[]{:S(2)}) async-start(bf16[128,24,1024]{2,1,0:T(8,128)(2,1)} %bitcast.215), calls=%async_computation.2 | async-start | bytes 12582912 | tf_op jit(solution)/shard_map/all_to_all | solution.py:82
  216.8 21.0 %slice-start.2 = ((s8[6291456]{0:T(1024)(128)(4,1)}), s8[2097152]{0:T(1024)(128)(4,1)S(1)}, s32[]{:S(2)}) async-start(s8[6291456]{0:T(1024)(128)(4,1)} %bitcast.227), calls=%async_computation.6 | async-start | bytes 4194304
  221.6 16.2 %slice-start.3 = ((s8[6291456]{0:T(1024)(128)(4,1)}), s8[4194304]{0:T(1024)(128)(4,1)S(1)}, s32[]{:S(2)}) async-start(s8[6291456]{0:T(1024)(128)(4,1)} %bitcast.227), calls=%async_computation.7 | async-start | bytes 8388608
  236.4 1.4 copy-start.14
  244.3 5.2 %copy-start.15 = (bf16[64,24,2,384]{3,1,2,0:T(8,128)(2,1)S(1)}, bf16[64,24,2,384]{3,1,2,0:T(8,128)(2,1)}, u32[]{:S(2)}) copy-start(bf16[64,24,2,384]{3,1,2,0:T(8,128)(2,1)} %copy-done.14) | copy-start | bytes 7077892
  249.5 4.3 %copy-start.10 = (bf16[2,2048,384]{2,1,0:T(8,128)(2,1)S(1)}, bf16[2,2048,384]{2,1,0:T(8,128)(2,1)}, u32[]{:S(2)}) copy-start(bf16[2,2048,384]{2,1,0:T(8,128)(2,1)} %param.10) | copy-start | bytes 9437188
  249.5 4.3 %copy-start.16 = (bf16[64,24,2,384]{3,1,2,0:T(8,128)(2,1)S(1)}, bf16[64,24,2,384]{3,1,2,0:T(8,128)(2,1)}, u32[]{:S(2)}) copy-start(bf16[64,24,2,384]{3,1,2,0:T(8,128)(2,1)} %copy-done.14) | copy-start | bytes 7077892
  253.8 2.8 copy-start.12
  253.8 2.7 copy-start.13
  285.2 89.3 %all-to-all-start.3 = ((bf16[128,24,1024]{2,1,0:T(8,128)(2,1)}), bf16[128,24,1024]{2,1,0:T(8,128)(2,1)}, u32[]{:S(2)}, u32[]{:S(2)}) async-start(bf16[128,24,1024]{2,1,0:T(8,128)(2,1)} %bitcast.213), calls=%async_computation.3 | async-start | bytes 12582912 | tf_op jit(solution)/shard_map/all_to_all | solution.py:82
  301.0 4.7 %copy-start.6 = (bf16[128,1024]{1,0:T(8,128)(2,1)S(1)}, bf16[128,1024]{1,0:T(8,128)(2,1)}, u32[]{:S(2)}) copy-start(bf16[128,1024]{1,0:T(8,128)(2,1)} %param.13) | copy-start | bytes 786436
  312.6 5.5 %copy-start.4 = (s32[128,8]{1,0:T(8,128)S(1)}, s32[128,8]{1,0:T(8,128)}, u32[]{:S(2)}) copy-start(s32[128,8]{1,0:T(8,128)} %copy-done.3) | copy-start | bytes 12292
  312.6 61.9 %copy-start.2 = (bf16[128,1536]{0,1:T(8,128)(2,1)S(1)}, bf16[128,1536]{0,1:T(8,128)(2,1)}, u32[]{:S(2)}) copy-start(bf16[128,1536]{0,1:T(8,128)(2,1)} %copy.80) | copy-start | bytes 1179652
  374.6 4.6 %copy-start.1 = (bf16[128,2048]{1,0:T(8,128)(2,1)S(1)}, bf16[128,2048]{1,0:T(8,128)(2,1)}, u32[]{:S(2)}) copy-start(bf16[128,2048]{1,0:T(8,128)(2,1)} %param.7) | copy-start | bytes 1572868
